TPU v7x, 32 devices: a whole 2x2x4 slice. The times are simulated.
32 devices in a mesh: grp: 4 (over x, core), tp: 8 (over z, y).
Axes of the slice: x: 2, y: 2, z: 4, core: 2. Of those that a mesh axis runs over, the one named last changes fastest.
Arguments:
- acts: bfloat16 [512, 8192], P('grp', 'tp'), may hold values from -6 to 6
- cotangent: bfloat16 [512, 8192], P('tp', 'grp'), may hold values from -18 to 18
- weight: bfloat16 [8192, 8192], P('tp', 'grp'), may hold values from -0.0625 to 0.0625
- moment: float32 [8192, 8192], P('tp', 'grp'), may hold values from -3 to 3
- second: float32 [8192, 8192], P('tp', 'grp'), may hold values from 0.05 to 1
- roll_acts: bfloat16 [64, 8192], P('grp', 'tp'), may hold values from -6 to 6
- live: int32 [4], P('grp'), may hold values from 4 to 16, as said below
Outputs:
- moment_new: float32 [8192, 8192], P('tp', 'grp')
- second_new: float32 [8192, 8192], P('tp', 'grp')
- prefill_out: bfloat16 [64, 8192], P('grp', 'tp')
Inputs may be any that keep to these rules, and one draw needn't show every extreme that they name: live slots of each replica's 16; some replica is full in every draw.
All inputs are finite; a program needn't handle non-finite values.
Results may differ from a plain program's by a relative error of at most 0.023.
Values may be sent and summed in bfloat16 or wider, within the bound.
No kernel may reach another device: no remote copies, remote signals or barrier semaphores. Data moves between devices by JAX's collectives and lax.ppermute only.
A program may use at most 128 MiB of HBM per device.

v0:
```python
import jax
import jax.numpy as jnp
from jax import lax
from jax.sharding import PartitionSpec as P

E = 8192
D = 8192
beta_one = 0.9
beta_two = 0.95
learn_rate = 0.003
weight_decay = 0.1
adam_eps = 1e-08
step_count = 10


def add_terms(left, right):
    return lax.dot_general(
        left, right, (((0,), (0,)), ((), ())), preferred_element_type=jnp.float32
    )


def shards(acts, cotangent, weight, moment, second, roll_acts, live):
    cot_full = lax.all_gather(cotangent, "tp", axis=0, tiled=True)
    grad = add_terms(lax.all_gather(acts, "grp", axis=0, tiled=True), cot_full)
    total_sq = lax.psum(jnp.sum(grad * grad), ("grp", "tp"))
    factor = jnp.minimum(1.0, 1.0 / jnp.sqrt(total_sq / (E * D) + 1e-06))
    clipped = grad * factor
    moment_new = beta_one * moment + (1.0 - beta_one) * clipped
    second_new = beta_two * second + (1.0 - beta_two) * clipped * clipped
    m_hat = moment_new / (1.0 - beta_one**step_count)
    v_hat = second_new / (1.0 - beta_two**step_count)
    old = weight.astype(jnp.float32)
    weight_new = (
        old - learn_rate * (m_hat / (jnp.sqrt(v_hat) + adam_eps) + weight_decay * old)
    ).astype(jnp.bfloat16)
    slot_count = roll_acts.shape[0]
    partial_sum = jnp.dot(
        roll_acts,
        lax.all_gather(weight_new, "grp", axis=1, tiled=True),
        preferred_element_type=jnp.float32,
    )
    summed = lax.psum_scatter(
        partial_sum.astype(jnp.bfloat16), "tp", scatter_dimension=1, tiled=True
    ).astype(jnp.float32)
    slots = lax.broadcasted_iota(jnp.int32, (slot_count, 1), 0)
    alive = slots < live[0]
    prefill_out = jnp.where(alive, summed, jnp.float32(0.0)).astype(jnp.bfloat16)
    return (moment_new, second_new, prefill_out)


def solution(mesh):
    placed = (
        P("grp", "tp"),
        P("tp", "grp"),
        P("tp", "grp"),
        P("tp", "grp"),
        P("tp", "grp"),
        P("grp", "tp"),
        P("grp"),
    )
    return jax.shard_map(
        shards,
        mesh=mesh,
        in_specs=placed,
        out_specs=(P("tp", "grp"), P("tp", "grp"), P("grp", "tp")),
        check_vma=False,
    )
```

profile of v0, /device:TPU:0, one launch (start us, length us, event | category | flops | bytes accessed | tf_op | source)
XLA Modules:
  0.0 332.5 jit_solution(6522618732154518133)
XLA Ops:
  7.2 0.0 copy-start
  7.2 0.0 all-gather.4.cloned.1.call-start
  7.2 0.7 all-gather.4.cloned.1.call-update
  7.9 0.0 all-gather.6.cloned.1.call-start
  8.0 0.7 all-gather.6.cloned.1.call-update
  8.7 0.0 all-gather.8.cloned.1.call-start
  8.7 20.3 %all-gather.4.cloned.1.call-done = bf16[512,1024]{1,0:T(8,128)(2,1)} async-done(((bf16[128,1024]{1,0:T(8,128)(2,1)}), bf16[512,1024]{1,0:T(8,128)(2,1)}) %all-gather.4.cloned.1.call-update) | async-done | bytes 1048592 | tf_op jit(solution)/shard_map/all_gather | solution.py:24
  29.0 51.2 %all-gather.6.cloned.1.call-done = bf16[512,2048]{1,0:T(8,128)(2,1)} async-done(((bf16[64,2048]{1,0:T(8,128)(2,1)}), bf16[512,2048]{1,0:T(8,128)(2,1)}) %all-gather.6.cloned.1.call-update) | async-done | bytes 2097168 | tf_op jit(solution)/shard_map/all_gather | solution.py:23
  80.2 8.3 %multiply_reduce_fusion = (f32[]{:T(128)}, f32[1024,2048]{1,0:T(8,128)}) fusion(bf16[512,1024]{1,0:T(8,128)(2,1)} %all-gather.4.cloned.1.call-done, bf16[512,2048]{1,0:T(8,128)(2,1)} %all-gather.6.cloned.1.call-done), kind=kOutput, calls=%fused_computation.10 | convolution fusion | flops 2151677952 | bytes 11534340 | tf_op jit(solution)/shard_map/dot_general | solution.py:17
  88.6 39.4 %psum.7 = f32[]{:T(128)} all-reduce(f32[]{:T(128)} %get-tuple-element.6), channel_id=1, replica_groups=mesh['grp'=4,'tp'=8] {'grp','tp'}, use_global_device_ids=true, to_apply=%region_1.0 | all-reduce | flops 1 | bytes 8 | tf_op jit(solution)/shard_map/psum | solution.py:25
  128.6 18.3 %fusion.3 = (bf16[1024,2048]{1,0:T(8,128)(2,1)}, f32[1024,2048]{1,0:T(8,128)}, f32[1024,2048]{1,0:T(8,128)}) fusion(bf16[1024,2048]{1,0:T(8,128)(2,1)} %param.9, f32[1024,2048]{1,0:T(8,128)} %get-tuple-element.7, f32[]{:T(128)S(6)} %min.3, f32[1024,2048]{1,0:T(8,128)} %param.11, f32[1024,2048]{1,0:T(8,128)} %param.10), kind=kLoop, calls=%fused_computation.7 | loop fusion | flops 37748736 | bytes 50331652 | tf_op jit(solution)/shard_map/convert_element_type | solution.py:35
  147.0 0.0 all-gather.8.cloned.1.call-update
  147.0 0.0 reduce-scatter.2.cloned.1.call-start
  147.1 106.5 %all-gather.8.cloned.1.call-done = bf16[1024,8192]{1,0:T(8,128)(2,1)} async-done(((bf16[1024,2048]{1,0:T(8,128)(2,1)}), bf16[1024,8192]{1,0:T(8,128)(2,1)}) %all-gather.8.cloned.1.call-update) | async-done | bytes 16777232 | tf_op jit(solution)/shard_map/all_gather | solution.py:39
  253.5 0.0 copy-done
  253.5 8.8 %fusion = bf16[16,8192]{1,0:T(8,128)(2,1)} fusion(bf16[16,1024]{1,0:T(8,128)(2,1)S(1)} %copy-done, bf16[1024,8192]{1,0:T(8,128)(2,1)} %all-gather.8.cloned.1.call-done), kind=kOutput, calls=%fused_computation.4 | convolution fusion | flops 268566528 | bytes 17072128 | tf_op jit(solution)/shard_map/dot_general | solution.py:37
  262.3 0.0 reduce-scatter.2.cloned.1.call-update
  263.0 61.6 %reduce-scatter.2.cloned.1.call-done = bf16[16,1024]{1,0:T(8,128)(2,1)} async-done(((bf16[16,8192]{1,0:T(8,128)(2,1)}), bf16[16,1024]{1,0:T(8,128)(2,1)}) %reduce-scatter.2.cloned.1.call-update) | async-done | bytes 32784 | tf_op jit(solution)/shard_map/reduce_scatter | solution.py:42
  324.6 1.4 select_convert_fusion
  (1 shorter events, 0.0 us)
Async XLA Ops:
  7.2 246.4 %copy-start = (bf16[16,1024]{1,0:T(8,128)(2,1)S(1)}, bf16[16,1024]{1,0:T(8,128)(2,1)}, u32[]{:S(2)}) copy-start(bf16[16,1024]{1,0:T(8,128)(2,1)} %param.12) | copy-start | bytes 98308
  7.2 21.8 %all-gather.4.cloned.1.call-start = ((), (), s32[]{:S(2)}) async-start(), calls=%async_computation.1 | async-start | bytes 1310720 | tf_op jit(solution)/shard_map/all_gather | solution.py:24
  7.9 72.3 %all-gather.6.cloned.1.call-start = ((), (), s32[]{:S(2)}) async-start(), calls=%async_computation.2 | async-start | bytes 2359296 | tf_op jit(solution)/shard_map/all_gather | solution.py:23
  8.7 244.9 %all-gather.8.cloned.1.call-start = ((), (), s32[]{:S(2)}) async-start(), calls=%async_computation.3 | async-start | bytes 20971520 | tf_op jit(solution)/shard_map/all_gather | solution.py:39
  147.0 177.5 %reduce-scatter.2.cloned.1.call-start = ((), (), s32[]{:S(2)}) async-start(), calls=%async_computation.4 | async-start | bytes 294912 | tf_op jit(solution)/shard_map/reduce_scatter | solution.py:42
Sparse Core Ops, SparseCore 0:
  9.5 19.4 all-gather.3
  31.1 49.0 all-gather.5
  147.1 106.3 all-gather.7
  262.4 62.0 reduce-scatter.1
where the time goes:
time: 333 us
  waiting for transfers between devices  241 us (72%)
  blocking collectives  39.4 us (12%)
  other arithmetic  19.8 us (6%)
  matrix products  17.1 us (5%)
  between operations  15.1 us (5%)
    all_gather x1, waiting for transfers between devices, shards(): lax.all_gather(weight_new, 'grp', axis=1, tiled=True)  106 us
    reduce_scatter x1, waiting for transfers between devices, shards(): lax.psum_scatter(partial_sum.astype(jnp.bfloat16), 'tp', scatter_dimensio...  61.6 us
    all_gather x1, waiting for transfers between devices, shards(): cot_full = lax.all_gather(cotangent, 'tp', axis=0, tiled=True)  51.2 us
    psum x1, blocking collectives, shards(): total_sq = lax.psum(jnp.sum(grad * grad), ('grp', 'tp'))  39.4 us
    all_gather x1, waiting for transfers between devices, shards(): grad = add_terms(lax.all_gather(acts, 'grp', axis=0, tiled=True), cot_full)  20.3 us
    convert_element_type x1, other arithmetic, shards(): weight_new = (old - learn_rate * (m_hat / (jnp.sqrt(v_hat) + adam_eps) +...  18.3 us
    dot_general x1, matrix products, shards(): jnp.dot(roll_acts, lax.all_gather(weight_new, 'grp', axis=1, tiled=True),...  8.77 us
    dot_general x1, matrix products, add_terms(): lax.dot_general(left, right, (((0,), (0,)), ((), ())), preferred_element_...  8.31 us
  transfers between devices with their start and end apart: 4, of which 4 were waited for; matrix products, arithmetic and copies ran while one was open for 0% of the time, Pallas kernels for 0%

commit v1 on v0

--- a/solution.py
+++ b/solution.py
@@ -1,3 +1,4 @@
+import functools
 import jax
 import jax.numpy as jnp
 from jax import lax
@@ -13,6 +14,26 @@
 step_count = 10
 
 
+def link_ticks(xx, named_axis):
+    tmp = lax.axis_size(named_axis)
+    row_out = lax.axis_index(named_axis)
+    o_now, taken_in, r_now = (tmp, row_out, xx.shape[0])
+    clean, z1 = (xx, 1)
+    while z1 < o_now:
+        answer = lax.ppermute(
+            clean,
+            axis_name=named_axis,
+            perm=[(dev_j, (dev_j - z1) % o_now) for dev_j in range(o_now)],
+        )
+        clean = jnp.concatenate([clean, answer], axis=0)
+        z1 = 2 * z1
+    plain = jnp.roll(clean, shift=taken_in * r_now, axis=0)
+    return plain
+
+
+list_the_seats_all = functools.partial(link_ticks, named_axis="grp")
+
+
 def add_terms(left, right):
     return lax.dot_general(
         left, right, (((0,), (0,)), ((), ())), preferred_element_type=jnp.float32
@@ -21,7 +42,7 @@
 
 def shards(acts, cotangent, weight, moment, second, roll_acts, live):
     cot_full = lax.all_gather(cotangent, "tp", axis=0, tiled=True)
-    grad = add_terms(lax.all_gather(acts, "grp", axis=0, tiled=True), cot_full)
+    grad = add_terms(list_the_seats_all(acts), cot_full)
     total_sq = lax.psum(jnp.sum(grad * grad), ("grp", "tp"))
     factor = jnp.minimum(1.0, 1.0 / jnp.sqrt(total_sq / (E * D) + 1e-06))
     clipped = grad * factor

time: 333 us -> 314 us (0.943)
  waiting for transfers between devices: 241 us -> 217 us
    all_gather x1, waiting for transfers between devices: 51.2 us -> 30.6 us  [shards(): cot_full = lax.all_gather(cotangent, 'tp', axis=0, tiled=True)]
    all_gather x1 -> x0, waiting for transfers between devices: 20.3 us -> none  [shards(): grad = add_terms(lax.all_gather(acts, 'grp', axis=0, tiled=True), cot_full)]
    ppermute x0 -> x2, waiting for transfers between devices: none -> 17.2 us  [link_ticks(): lax.ppermute(clean, axis_name=named_axis, perm=[(dev_j, (dev_j - z1) % o_...]
  transfers between devices with their start and end apart: 4 -> 5, of which waited for: 4 -> 5; matrix products, arithmetic and copies ran while one was open for 0% -> 1% of each run, Pallas kernels for 0% -> 0%
where the time goes in v1:
time: 314 us
  waiting for transfers between devices  217 us (69%)
  blocking collectives  39.4 us (13%)
  other arithmetic  20.8 us (7%)
  matrix products  16.7 us (5%)
  between operations  15.1 us (5%)
  starting transfers between devices  3.21 us (1%)
    all_gather x1, waiting for transfers between devices, shards(): lax.all_gather(weight_new, 'grp', axis=1, tiled=True)  106 us
    reduce_scatter x1, waiting for transfers between devices, shards(): lax.psum_scatter(partial_sum.astype(jnp.bfloat16), 'tp', scatter_dimensio...  61.6 us
    psum x1, blocking collectives, shards(): total_sq = lax.psum(jnp.sum(grad * grad), ('grp', 'tp'))  39.4 us
    all_gather x1, waiting for transfers between devices, shards(): cot_full = lax.all_gather(cotangent, 'tp', axis=0, tiled=True)  30.6 us
    convert_element_type x1, other arithmetic, shards(): weight_new = (old - learn_rate * (m_hat / (jnp.sqrt(v_hat) + adam_eps) +...  18.3 us
    ppermute x2, waiting for transfers between devices, link_ticks(): lax.ppermute(clean, axis_name=named_axis, perm=[(dev_j, (dev_j - z1) % o_...  17.2 us
    dot_general x1, matrix products, shards(): jnp.dot(roll_acts, lax.all_gather(weight_new, 'grp', axis=1, tiled=True),...  8.77 us
    dot_general x1, matrix products, add_terms(): lax.dot_general(left, right, (((0,), (0,)), ((), ())), preferred_element_...  7.98 us
  transfers between devices with their start and end apart: 5, of which 5 were waited for; matrix products, arithmetic and copies ran while one was open for 1% of the time, Pallas kernels for 0%

profile of v1, /device:TPU:0, one launch (start us, length us, event | category | flops | bytes accessed | tf_op | source)
XLA Modules:
  0.0 313.9 jit_solution(9192174021277609644)
XLA Ops:
  7.2 0.0 copy-start
  7.2 0.0 all-gather.3.cloned.1.call-start
  7.2 0.7 all-gather.3.cloned.1.call-update
  7.9 0.0 all-gather.5.cloned.1.call-start
  8.0 2.5 collective-permute-start
  10.4 4.2 %collective-permute-done = bf16[128,1024]{1,0:T(8,128)(2,1)S(1)} collective-permute-done((bf16[128,1024]{1,0:T(8,128)(2,1)}, bf16[128,1024]{1,0:T(8,128)(2,1)S(1)}, u32[]{:S(2)}, u32[]{:S(2)}) %collective-permute-start) | collective-permute-done | bytes 262176 | tf_op jit(solution)/shard_map/ppermute | solution.py:23
  14.6 1.0 pad_maximum_fusion
  15.6 0.6 collective-permute-start.1
  16.2 1.0 constant_dynamic-update-slice_fusion.5
  17.2 13.0 %collective-permute-done.1 = bf16[256,1024]{1,0:T(8,128)(2,1)S(1)} collective-permute-done((bf16[256,1024]{1,0:T(8,128)(2,1)S(1)}, bf16[256,1024]{1,0:T(8,128)(2,1)S(1)}, u32[]{:S(2)}, u32[]{:S(2)}) %collective-permute-start.1) | collective-permute-done | bytes 524320 | tf_op jit(solution)/shard_map/ppermute | solution.py:23
  30.3 1.0 constant_dynamic-update-slice_fusion.2
  31.3 30.6 %all-gather.3.cloned.1.call-done = bf16[512,2048]{1,0:T(8,128)(2,1)} async-done(((bf16[64,2048]{1,0:T(8,128)(2,1)}), bf16[512,2048]{1,0:T(8,128)(2,1)}) %all-gather.3.cloned.1.call-update) | async-done | bytes 2097168 | tf_op jit(solution)/shard_map/all_gather | solution.py:44
  62.0 8.0 %multiply_reduce_fusion = (f32[]{:T(128)}, f32[1024,2048]{1,0:T(8,128)}) fusion(bf16[512,2048]{1,0:T(8,128)(2,1)} %all-gather.3.cloned.1.call-done, bf16[1024,1024]{1,0:T(8,128)(2,1)S(1)} %constant_dynamic-update-slice_fusion, s32[]{:T(128)S(6)} %select_n.18), kind=kOutput, calls=%fused_computation.10 | convolution fusion | flops 2151677952 | bytes 11534344 | tf_op jit(solution)/shard_map/dot_general | solution.py:38
  69.9 39.4 %psum.7 = f32[]{:T(128)} all-reduce(f32[]{:T(128)} %get-tuple-element.6), channel_id=1, replica_groups=mesh['grp'=4,'tp'=8] {'grp','tp'}, use_global_device_ids=true, to_apply=%region_1.2 | all-reduce | flops 1 | bytes 8 | tf_op jit(solution)/shard_map/psum | solution.py:46
  110.0 18.3 %fusion.3 = (bf16[1024,2048]{1,0:T(8,128)(2,1)}, f32[1024,2048]{1,0:T(8,128)}, f32[1024,2048]{1,0:T(8,128)}) fusion(bf16[1024,2048]{1,0:T(8,128)(2,1)} %param.9, f32[1024,2048]{1,0:T(8,128)} %get-tuple-element.7, f32[]{:T(128)S(6)} %min.3, f32[1024,2048]{1,0:T(8,128)} %param.11, f32[1024,2048]{1,0:T(8,128)} %param.10), kind=kLoop, calls=%fused_computation.7 | loop fusion | flops 37748736 | bytes 50331652 | tf_op jit(solution)/shard_map/convert_element_type | solution.py:56
  128.3 0.0 all-gather.5.cloned.1.call-update
  128.4 0.0 reduce-scatter.2.cloned.1.call-start
  128.4 106.5 %all-gather.5.cloned.1.call-done = bf16[1024,8192]{1,0:T(8,128)(2,1)} async-done(((bf16[1024,2048]{1,0:T(8,128)(2,1)}), bf16[1024,8192]{1,0:T(8,128)(2,1)}) %all-gather.5.cloned.1.call-update) | async-done | bytes 16777232 | tf_op jit(solution)/shard_map/all_gather | solution.py:60
  234.9 0.0 copy-done
  234.9 8.8 %fusion = bf16[16,8192]{1,0:T(8,128)(2,1)} fusion(bf16[16,1024]{1,0:T(8,128)(2,1)S(1)} %copy-done, bf16[1024,8192]{1,0:T(8,128)(2,1)} %all-gather.5.cloned.1.call-done), kind=kOutput, calls=%fused_computation.4 | convolution fusion | flops 268566528 | bytes 17072128 | tf_op jit(solution)/shard_map/dot_general | solution.py:58
  243.6 0.0 reduce-scatter.2.cloned.1.call-update
  244.3 61.6 %reduce-scatter.2.cloned.1.call-done = bf16[16,1024]{1,0:T(8,128)(2,1)} async-done(((bf16[16,8192]{1,0:T(8,128)(2,1)}), bf16[16,1024]{1,0:T(8,128)(2,1)}) %reduce-scatter.2.cloned.1.call-update) | async-done | bytes 32784 | tf_op jit(solution)/shard_map/reduce_scatter | solution.py:63
  305.9 1.4 select_convert_fusion
  (5 shorter events, 0.1 us)
Async XLA Ops:
  7.2 227.7 %copy-start = (bf16[16,1024]{1,0:T(8,128)(2,1)S(1)}, bf16[16,1024]{1,0:T(8,128)(2,1)}, u32[]{:S(2)}) copy-start(bf16[16,1024]{1,0:T(8,128)(2,1)} %param.12) | copy-start | bytes 98308
  7.2 54.8 %all-gather.3.cloned.1.call-start = ((), (), s32[]{:S(2)}) async-start(), calls=%async_computation.1 | async-start | bytes 2359296 | tf_op jit(solution)/shard_map/all_gather | solution.py:44
  7.9 227.0 %all-gather.5.cloned.1.call-start = ((), (), s32[]{:S(2)}) async-start(), calls=%async_computation.2 | async-start | bytes 20971520 | tf_op jit(solution)/shard_map/all_gather | solution.py:60
  8.0 6.7 %collective-permute-start = (bf16[128,1024]{1,0:T(8,128)(2,1)}, bf16[128,1024]{1,0:T(8,128)(2,1)S(1)}, u32[]{:S(2)}, u32[]{:S(2)}) collective-permute-start(bf16[128,1024]{1,0:T(8,128)(2,1)} %param.7), channel_id=1, source_target_pairs={{0,24},{8,0},{16,8},{24,16},{1,25},{9,1},{17,9},{25,17},{2,26},{10... | collective-permute-start | bytes 786440 | tf_op jit(solution)/shard_map/ppermute | solution.py:23
  15.6 14.6 %collective-permute-start.1 = (bf16[256,1024]{1,0:T(8,128)(2,1)S(1)}, bf16[256,1024]{1,0:T(8,128)(2,1)S(1)}, u32[]{:S(2)}, u32[]{:S(2)}) collective-permute-start(bf16[256,1024]{1,0:T(8,128)(2,1)S(1)} %pad_maximum_fusion), channel_id=1, source_target_pairs={{0,16},{8,24},{16,0},{24,8},{1,17},{9,25},{17,1},{25,9},{2,18},{10... | collective-permute-start | bytes 1572872 | tf_op jit(solution)/shard_map/ppermute | solution.py:23
  128.4 177.5 %reduce-scatter.2.cloned.1.call-start = ((), (), s32[]{:S(2)}) async-start(), calls=%async_computation.3 | async-start | bytes 294912 | tf_op jit(solution)/shard_map/reduce_scatter | solution.py:63
Sparse Core Ops, SparseCore 0:
  10.1 51.7 all-gather.2
  128.5 106.3 all-gather.4
  243.8 62.0 reduce-scatter.1
